TPU v7x, 128 devices: a whole 4x4x4 slice. The times are simulated.
128 devices in a mesh: width: 4 (over z), row: 4 (over y), src: 8 (over x, core).
Axes of the slice: x: 4, y: 4, z: 4, core: 2. Of those that a mesh axis runs over, the one named last changes fastest.
Arguments:
- query_rows: bfloat16 [1024, 8192], P('row', 'width'), may hold values from -150 to 150
- key_rows: bfloat16 [1024, 1024], P('src', 'width'), may hold values from -7 to 7
- value_rows: bfloat16 [1024, 1024], P('src'), may hold values from -6 to 6
- out_proj: bfloat16 [8192, 8192], P(('row', 'src'), 'width'), may hold values from -0.0625 to 0.0625
Outputs:
- share: float32 [1024, 1024], P('row', ('src', 'width'))
All inputs are finite; a program needn't handle non-finite values.
Results may differ from a plain program's by a relative error of at most 0.0014.
Values may be sent and summed in bfloat16 or wider, within the bound.
A program may use at most 192 MiB of HBM per device.

v0:
```python
import math
import jax
import jax.numpy as jnp
from jax import lax
from jax.sharding import PartitionSpec as P

H = 64
KV = 8
HD = 128


def sent_to_all(shard, axis):
    copies = jnp.broadcast_to(shard, (lax.axis_size(axis), *shard.shape))
    return lax.all_to_all(copies, axis, split_axis=0, concat_axis=0, tiled=True)


def gathered_once(shard, axis):
    leaves = jax.tree.leaves(shard)
    sequence = sorted(range(len(leaves)), key=lambda k: -leaves[k].size)
    width = (1, *leaves[sequence[0]].shape)[-1]
    lines = [
        jnp.pad(leaves[k].reshape(-1), (0, -leaves[k].size % width)).reshape(-1, width)
        for k in sequence
    ]
    both, at, found = (sent_to_all(jnp.concatenate(lines), axis), 0, {})
    for k, line in zip(sequence, lines):
        slab = both[:, at : at + len(line)].reshape(len(both), -1)
        found[k] = slab[:, : leaves[k].size].reshape(-1, *leaves[k].shape)
        at += len(line)
    numbers = iter(range(len(leaves)))
    return jax.tree.map(lambda _: found[next(numbers)], shard)


def combined_pairwise(pieces, combine):
    while len(jax.tree.leaves(pieces)[0]) > 1:
        pieces = jax.vmap(combine)(
            *(jax.tree.map(lambda part: part[side::2], pieces) for side in (0, 1))
        )
    return jax.tree.map(lambda part: part[0], pieces)


def merged(shard, axis, combine):
    pieces = gathered_once(shard, axis)
    return combined_pairwise(pieces, combine)


def cut_along(shard, dim, size):
    dims = shard.shape
    parts = shard.reshape(*dims[:dim], size, dims[dim] // size, *dims[dim + 1 :])
    return jnp.moveaxis(parts, dim, 0)


def sum_at_owner(shard, axis, dim):
    size = lax.axis_size(axis)
    parts = lax.all_to_all(cut_along(shard, dim, size), axis, 0, 0, tiled=True)
    return jnp.sum(parts, axis=0)


def of_everyone(shard, axis):
    return sent_to_all(shard, axis).sum(axis=0)


def combine_stats(first, second):
    peak_one, mass_one = first
    peak_two, mass_two = second
    larger = jnp.maximum(peak_one, peak_two)
    return (larger, mass_one * jnp.exp(peak_one - larger) + mass_two * jnp.exp(peak_two - larger))


def body(query_rows, key_rows, value_rows, out_proj):
    here_row = lax.axis_index("row")
    here_src = lax.axis_index("src")
    row_count = query_rows.shape[0]
    col_count = key_rows.shape[0]
    group_size = H // KV
    row_pos = here_row * row_count + jnp.arange(row_count, dtype=jnp.int32)
    col_pos = here_src * col_count + jnp.arange(col_count, dtype=jnp.int32)
    local_heads = query_rows.shape[1] // HD
    local_kv = key_rows.shape[1] // HD
    queries = query_rows.reshape(row_count, local_kv, group_size, HD)
    key_heads = key_rows.reshape(col_count, local_kv, HD)
    scores = jnp.einsum("ikgd,jkd->kgij", queries, key_heads, preferred_element_type=jnp.float32)
    scores = scores.reshape(local_heads, row_count, col_count) / jnp.sqrt(jnp.float32(HD))
    causal = row_pos[:, None] >= col_pos[None, :]
    masked = jnp.where(causal, scores, jnp.float32(-1e30))
    row_peak = jnp.max(masked, axis=-1)
    row_mass = jnp.sum(jnp.where(causal, jnp.exp(masked - row_peak[..., None]), 0.0), axis=-1)
    row_peak, row_mass = merged((row_peak, row_mass), "src", combine_stats)
    weights = jnp.where(
        causal, jnp.exp(masked - row_peak[..., None]) / row_mass[..., None], 0.0
    ).astype(jnp.bfloat16)
    weights = lax.all_gather(weights, "width", axis=0, tiled=True)
    value_heads = value_rows.reshape(col_count, KV, HD)
    out_cols = out_proj.shape[1]
    proj_heads = out_proj.reshape(-1, HD, out_cols)
    portion = lax.all_gather(proj_heads, ("row", "src"), axis=0, tiled=True)
    head_count = portion.shape[0]
    head_ids = jnp.arange(head_count, dtype=jnp.int32)
    selector = (head_ids[:, None] // group_size == jnp.arange(KV, dtype=jnp.int32)[None, :]).astype(
        jnp.bfloat16
    )
    chosen = jnp.einsum(
        "hk,jkd->jhd", selector, value_heads, preferred_element_type=jnp.float32
    ).astype(jnp.bfloat16)
    images = jnp.einsum("jhd,hde->jhe", chosen, portion, preferred_element_type=jnp.float32).astype(
        jnp.bfloat16
    )
    row_block = math.gcd(row_count, 64)
    col_block = math.gcd(col_count, 32)
    col_steps = col_count // col_block
    turns = row_count // row_block * col_steps

    def tile(turn_index, running):
        row_start = turn_index // col_steps * row_block
        col_start = turn_index % col_steps * col_block
        row_slice = lax.dynamic_slice_in_dim(row_pos, row_start, row_block)
        col_slice = lax.dynamic_slice_in_dim(col_pos, col_start, col_block)

        def compute(unused):
            attend = lax.dynamic_slice(
                weights, (0, row_start, col_start), (H, row_block, col_block)
            )
            source_images = lax.dynamic_slice_in_dim(images, col_start, col_block, 0)
            contrib = jnp.einsum(
                "hij,jhe->ije", attend, source_images, preferred_element_type=jnp.float32
            )
            return jnp.sum(jnp.abs(contrib), axis=-1)

        def skipped(unused):
            return jnp.zeros((row_block, col_block), jnp.float32)

        result = lax.cond(jnp.max(row_slice) >= jnp.min(col_slice), compute, skipped, 0)
        return lax.dynamic_update_slice(running, result, (row_start, col_start))

    partial_value = lax.fori_loop(0, turns, tile, jnp.zeros((row_count, col_count), jnp.float32))
    summed = sum_at_owner(partial_value, "width", 1)
    totals = of_everyone(jnp.sum(summed, axis=1), ("width", "src"))
    position = (here_row * row_count + jnp.arange(row_count, dtype=jnp.int32) + 1).astype(
        jnp.float32
    )
    return position[:, None] * summed / totals[:, None]


def solution(mesh):
    placed = (P("row", "width"), P("src", "width"), P("src", None), P(("row", "src"), "width"))
    return jax.shard_map(
        body, mesh=mesh, in_specs=placed, out_specs=P("row", ("src", "width")), check_vma=False
    )
```

profile of v0, /device:TPU:25, one launch (start us, length us, event | category | flops | bytes accessed | tf_op | source)
XLA Modules:
  0.0 431.4 jit_solution(18067964968503341397)
XLA Ops:
  27.2 47.7 %all-gather.5.cloned.1.call-done = bf16[64,256,128]{2,1,0:T(8,128)(2,1)} async-done(((bf16[16,256,128]{2,1,0:T(8,128)(2,1)}), bf16[64,256,128]{2,1,0:T(8,128)(2,1)}) %all-gather.5.cloned.1.call-update) | async-done | bytes 4194320 | tf_op jit(solution)/shard_map/all_gather | solution.py:92
  75.0 15.6 %copy.29 = bf16[64,256,128]{0,1,2:T(8,128)(2,1)} copy(bf16[64,256,128]{2,1,0:T(8,128)(2,1)} %all-gather.5.cloned.1.call-done) | data formatting | bytes 8388608 | tf_op jit(solution)/shard_map/while | solution.py:135
  90.6 100.2 %all-gather.3.cloned.1.call-done = bf16[64,128,2048]{2,1,0:T(8,128)(2,1)} async-done(((bf16[2,128,2048]{2,1,0:T(8,128)(2,1)}), bf16[64,128,2048]{2,1,0:T(8,128)(2,1)}) %all-gather.3.cloned.1.call-update) | async-done | bytes 33554448 | tf_op jit(solution)/shard_map/all_gather | solution.py:96
  190.8 24.2 %convert_bitcast_fusion = bf16[128,64,2048]{2,0,1:T(8,128)(2,1)} fusion(bf16[64,128,2048]{2,1,0:T(8,128)(2,1)} %all-gather.3.cloned.1.call-done, bf16[128,64,128]{2,1,0:T(8,128)(2,1)S(1)} %convert_bitcast_fusion.1), kind=kOutput, calls=%fused_computation.7 | convolution fusion | flops 4311744512 | bytes 69206016 | tf_op jit(solution)/shard_map/jhd,hde->jhe/dot_general | solution.py:105
  215.0 30.0 %copy.28 = bf16[128,64,2048]{2,1,0:T(8,128)(2,1)} copy(bf16[128,64,2048]{2,0,1:T(8,128)(2,1)} %convert_bitcast_fusion) | data formatting | bytes 67108864 | tf_op jit(solution)/shard_map/while | solution.py:135
  245.0 156.7 %while.15 = (s32[]{:T(128)}, f32[256,128]{0,1:T(8,128)S(1)}, s32[256]{0:T(256)S(1)}, s32[128]{0:T(128)S(1)}, bf16[128,64,2048]{2,1,0:T(8,128)(2,1)}, /*index=5*/...) while((s32[]{:T(128)}, f32[256,128]{0,1:T(8,128)S(1)}, ...), condition=%wide.region_8.9_spmd, body=%wide.region_2.8_spmd.sunk | while | flops 545257600 | bytes 8939898 | solution.py:135
  247.9 6.0 %conditional.2 = (f32[64,32]{0,1:T(8,128)S(1)}) conditional(s32[]{:T(128)} %convert_element_type.44, () %tuple.54, (s32[]{:T(128)}, bf16[128,64,2048]{2,1,0:T(8,128)(2,1)}, s32[]{:T(128)}, bf16[64,256,128]{0,1,2:T(8,128)(2,1)}) %tuple.55), branch_computations={%region_5.5_spmd, %region_6.7_spmd} | conditional | flops 545257472 | bytes 8922700 | solution.py:132
  257.7 6.0 %conditional.2 = (f32[64,32]{0,1:T(8,128)S(1)}) conditional(s32[]{:T(128)} %convert_element_type.44, () %tuple.54, (s32[]{:T(128)}, bf16[128,64,2048]{2,1,0:T(8,128)(2,1)}, s32[]{:T(128)}, bf16[64,256,128]{0,1,2:T(8,128)(2,1)}) %tuple.55), branch_computations={%region_5.5_spmd, %region_6.7_spmd} | conditional | flops 545257472 | bytes 8922700 | solution.py:132
  267.5 6.0 %conditional.2 = (f32[64,32]{0,1:T(8,128)S(1)}) conditional(s32[]{:T(128)} %convert_element_type.44, () %tuple.54, (s32[]{:T(128)}, bf16[128,64,2048]{2,1,0:T(8,128)(2,1)}, s32[]{:T(128)}, bf16[64,256,128]{0,1,2:T(8,128)(2,1)}) %tuple.55), branch_computations={%region_5.5_spmd, %region_6.7_spmd} | conditional | flops 545257472 | bytes 8922700 | solution.py:132
  277.3 6.0 %conditional.2 = (f32[64,32]{0,1:T(8,128)S(1)}) conditional(s32[]{:T(128)} %convert_element_type.44, () %tuple.54, (s32[]{:T(128)}, bf16[128,64,2048]{2,1,0:T(8,128)(2,1)}, s32[]{:T(128)}, bf16[64,256,128]{0,1,2:T(8,128)(2,1)}) %tuple.55), branch_computations={%region_5.5_spmd, %region_6.7_spmd} | conditional | flops 545257472 | bytes 8922700 | solution.py:132
  286.9 6.0 %conditional.2 = (f32[64,32]{0,1:T(8,128)S(1)}) conditional(s32[]{:T(128)} %convert_element_type.44, () %tuple.54, (s32[]{:T(128)}, bf16[128,64,2048]{2,1,0:T(8,128)(2,1)}, s32[]{:T(128)}, bf16[64,256,128]{0,1,2:T(8,128)(2,1)}) %tuple.55), branch_computations={%region_5.5_spmd, %region_6.7_spmd} | conditional | flops 545257472 | bytes 8922700 | solution.py:132
  297.0 6.0 %conditional.2 = (f32[64,32]{0,1:T(8,128)S(1)}) conditional(s32[]{:T(128)} %convert_element_type.44, () %tuple.54, (s32[]{:T(128)}, bf16[128,64,2048]{2,1,0:T(8,128)(2,1)}, s32[]{:T(128)}, bf16[64,256,128]{0,1,2:T(8,128)(2,1)}) %tuple.55), branch_computations={%region_5.5_spmd, %region_6.7_spmd} | conditional | flops 545257472 | bytes 8922700 | solution.py:132
  307.0 6.0 %conditional.2 = (f32[64,32]{0,1:T(8,128)S(1)}) conditional(s32[]{:T(128)} %convert_element_type.44, () %tuple.54, (s32[]{:T(128)}, bf16[128,64,2048]{2,1,0:T(8,128)(2,1)}, s32[]{:T(128)}, bf16[64,256,128]{0,1,2:T(8,128)(2,1)}) %tuple.55), branch_computations={%region_5.5_spmd, %region_6.7_spmd} | conditional | flops 545257472 | bytes 8922700 | solution.py:132
  317.1 6.0 %conditional.2 = (f32[64,32]{0,1:T(8,128)S(1)}) conditional(s32[]{:T(128)} %convert_element_type.44, () %tuple.54, (s32[]{:T(128)}, bf16[128,64,2048]{2,1,0:T(8,128)(2,1)}, s32[]{:T(128)}, bf16[64,256,128]{0,1,2:T(8,128)(2,1)}) %tuple.55), branch_computations={%region_5.5_spmd, %region_6.7_spmd} | conditional | flops 545257472 | bytes 8922700 | solution.py:132
  327.0 6.0 %conditional.2 = (f32[64,32]{0,1:T(8,128)S(1)}) conditional(s32[]{:T(128)} %convert_element_type.44, () %tuple.54, (s32[]{:T(128)}, bf16[128,64,2048]{2,1,0:T(8,128)(2,1)}, s32[]{:T(128)}, bf16[64,256,128]{0,1,2:T(8,128)(2,1)}) %tuple.55), branch_computations={%region_5.5_spmd, %region_6.7_spmd} | conditional | flops 545257472 | bytes 8922700 | solution.py:132
  336.6 6.0 %conditional.2 = (f32[64,32]{0,1:T(8,128)S(1)}) conditional(s32[]{:T(128)} %convert_element_type.44, () %tuple.54, (s32[]{:T(128)}, bf16[128,64,2048]{2,1,0:T(8,128)(2,1)}, s32[]{:T(128)}, bf16[64,256,128]{0,1,2:T(8,128)(2,1)}) %tuple.55), branch_computations={%region_5.5_spmd, %region_6.7_spmd} | conditional | flops 545257472 | bytes 8922700 | solution.py:132
  346.2 6.0 %conditional.2 = (f32[64,32]{0,1:T(8,128)S(1)}) conditional(s32[]{:T(128)} %convert_element_type.44, () %tuple.54, (s32[]{:T(128)}, bf16[128,64,2048]{2,1,0:T(8,128)(2,1)}, s32[]{:T(128)}, bf16[64,256,128]{0,1,2:T(8,128)(2,1)}) %tuple.55), branch_computations={%region_5.5_spmd, %region_6.7_spmd} | conditional | flops 545257472 | bytes 8922700 | solution.py:132
  355.8 6.0 %conditional.2 = (f32[64,32]{0,1:T(8,128)S(1)}) conditional(s32[]{:T(128)} %convert_element_type.44, () %tuple.54, (s32[]{:T(128)}, bf16[128,64,2048]{2,1,0:T(8,128)(2,1)}, s32[]{:T(128)}, bf16[64,256,128]{0,1,2:T(8,128)(2,1)}) %tuple.55), branch_computations={%region_5.5_spmd, %region_6.7_spmd} | conditional | flops 545257472 | bytes 8922700 | solution.py:132
  365.2 6.0 %conditional.2 = (f32[64,32]{0,1:T(8,128)S(1)}) conditional(s32[]{:T(128)} %convert_element_type.44, () %tuple.54, (s32[]{:T(128)}, bf16[128,64,2048]{2,1,0:T(8,128)(2,1)}, s32[]{:T(128)}, bf16[64,256,128]{0,1,2:T(8,128)(2,1)}) %tuple.55), branch_computations={%region_5.5_spmd, %region_6.7_spmd} | conditional | flops 545257472 | bytes 8922700 | solution.py:132
  375.1 6.0 %conditional.2 = (f32[64,32]{0,1:T(8,128)S(1)}) conditional(s32[]{:T(128)} %convert_element_type.44, () %tuple.54, (s32[]{:T(128)}, bf16[128,64,2048]{2,1,0:T(8,128)(2,1)}, s32[]{:T(128)}, bf16[64,256,128]{0,1,2:T(8,128)(2,1)}) %tuple.55), branch_computations={%region_5.5_spmd, %region_6.7_spmd} | conditional | flops 545257472 | bytes 8922700 | solution.py:132
  384.9 6.0 %conditional.2 = (f32[64,32]{0,1:T(8,128)S(1)}) conditional(s32[]{:T(128)} %convert_element_type.44, () %tuple.54, (s32[]{:T(128)}, bf16[128,64,2048]{2,1,0:T(8,128)(2,1)}, s32[]{:T(128)}, bf16[64,256,128]{0,1,2:T(8,128)(2,1)}) %tuple.55), branch_computations={%region_5.5_spmd, %region_6.7_spmd} | conditional | flops 545257472 | bytes 8922700 | solution.py:132
  394.8 6.0 %conditional.2 = (f32[64,32]{0,1:T(8,128)S(1)}) conditional(s32[]{:T(128)} %convert_element_type.44, () %tuple.54, (s32[]{:T(128)}, bf16[128,64,2048]{2,1,0:T(8,128)(2,1)}, s32[]{:T(128)}, bf16[64,256,128]{0,1,2:T(8,128)(2,1)}) %tuple.55), branch_computations={%region_5.5_spmd, %region_6.7_spmd} | conditional | flops 545257472 | bytes 8922700 | solution.py:132
  401.7 8.7 %all_to_all.16 = f32[4,256,32]{1,2,0:T(8,128)S(1)} all-to-all(f32[4,256,32]{1,2,0:T(8,128)S(1)} %bitcast.40), channel_id=1, replica_groups=mesh['width'=4,'row'=4,'src'=8] {'width'}, dimensions={0} | all-to-all | bytes 262144 | tf_op jit(solution)/shard_map/all_to_all | solution.py:55
  416.6 7.2 %all-to-all-done.2 = f32[32,1,256]{2,1,0:T(1,128)S(1)} async-done(((f32[32,1,256]{2,1,0:T(1,128)}), f32[32,1,256]{2,1,0:T(1,128)S(1)}, u32[]{:S(2)}, u32[]{:S(2)}) %all-to-all-start.2) | async-done | bytes 32800 | tf_op jit(solution)/shard_map/all_to_all | solution.py:14
  (100 shorter events, 161.9 us)
Async XLA Ops:
  6.5 1.5 copy-start.1
  10.0 11.5 %all-to-all-start = ((f32[8,32,256]{2,1,0:T(8,128)}), f32[8,32,256]{2,1,0:T(8,128)S(1)}, u32[]{:S(2)}, u32[]{:S(2)}) async-start(f32[8,32,256]{2,1,0:T(8,128)} %broadcast_in_dim.44), calls=%async_computation | async-start | bytes 524288 | tf_op jit(solution)/shard_map/all_to_all | solution.py:14
  14.9 60.0 %all-gather.5.cloned.1.call-start = ((), (), s32[]{:S(2)}) async-start(), calls=%async_computation.4 | async-start | bytes 5242880 | tf_op jit(solution)/shard_map/all_gather | solution.py:92
  21.6 4.9 %copy-start = (bf16[128,1024]{1,0:T(8,128)(2,1)S(1)}, bf16[128,1024]{1,0:T(8,128)(2,1)}, u32[]{:S(2)}) copy-start(bf16[128,1024]{1,0:T(8,128)(2,1)} %param.10) | copy-start | bytes 786436
  25.7 165.1 %all-gather.3.cloned.1.call-start = ((), (), s32[]{:S(2)}) async-start(), calls=%async_computation.3 | async-start | bytes 34603008 | tf_op jit(solution)/shard_map/all_gather | solution.py:96
  411.1 12.8 %all-to-all-start.2 = ((f32[32,1,256]{2,1,0:T(1,128)}), f32[32,1,256]{2,1,0:T(1,128)S(1)}, u32[]{:S(2)}, u32[]{:S(2)}) async-start(f32[32,1,256]{2,1,0:T(1,128)} %broadcast_in_dim.46), calls=%async_computation.2 | async-start | bytes 65536 | tf_op jit(solution)/shard_map/all_to_all | solution.py:14
Sparse Core Ops, SparseCore 0:
  25.8 49.1 all-gather.4
  77.2 113.4 all-gather.2
where the time goes:
time: 432 us; the launch traced here: 431 us
  waiting for transfers between devices  160 us (37%)
  matrix products  122 us (28%)
  local copies, waits for them, and re-layouts  64.2 us (15%)
  other arithmetic  30.2 us (7%)
  loops' own time  22.2 us (5%)
  between operations  13.6 us (3%)
  starting transfers between devices  10.8 us (2%)
  blocking collectives  8.75 us (2%)
    all_gather x1, waiting for transfers between devices, body(): portion = lax.all_gather(proj_heads, ('row', 'src'), axis=0, tiled=True)  100 us
    dot_general x16, matrix products, compute(): jnp.einsum('hij,jhe->ije', attend, source_images, preferred_element_type=...  96.1 us
    all_gather x1, waiting for transfers between devices, body(): weights = lax.all_gather(weights, 'width', axis=0, tiled=True)  47.7 us
    while x2, local copies, waits for them, and re-layouts, body(): lax.fori_loop(0, turns, tile, jnp.zeros((row_count, col_count), jnp.float...  45.6 us
    dot_general x1, matrix products, body(): jnp.einsum('jhd,hde->jhe', chosen, portion, preferred_element_type=jnp.fl...  24.2 us
    another operation x1, loops' own time, body(): lax.fori_loop(0, turns, tile, jnp.zeros((row_count, col_count), jnp.float...  21.8 us
    dynamic_update_slice x16, local copies, waits for them, and re-layouts, tile(): return lax.dynamic_update_slice(running, result, (row_start, col_start))  13.7 us
    reduce_max x16, other arithmetic, tile(): jnp.max(row_slice) >= jnp.min(col_slice)  12.5 us
  transfers between devices with their start and end apart: 4, of which 4 were waited for; matrix products, arithmetic and copies ran while one was open for 4% of the time, Pallas kernels for 0%

commit v1 on v0

--- a/solution.py
+++ b/solution.py
@@ -89,7 +89,13 @@
     weights = jnp.where(
         causal, jnp.exp(masked - row_peak[..., None]) / row_mass[..., None], 0.0
     ).astype(jnp.bfloat16)
-    weights = lax.all_gather(weights, "width", axis=0, tiled=True)
+    n_dev = lax.axis_size("width")
+    held, shards = (weights, [weights])
+    for _ in range(n_dev - 1):
+        held = lax.ppermute(held, "width", [(i, (i + 1) % n_dev) for i in range(n_dev)])
+        shards.insert(0, held)
+    row_of_blocks = jnp.concatenate(shards, axis=0)
+    weights = jnp.roll(row_of_blocks, (lax.axis_index("width") + 1) * weights.shape[0], axis=0)
     value_heads = value_rows.reshape(col_count, KV, HD)
     out_cols = out_proj.shape[1]
     proj_heads = out_proj.reshape(-1, HD, out_cols)

time: 432 us -> 369 us (0.85)
  waiting for transfers between devices: 160 us -> 81.8 us
  local copies, waits for them, and re-layouts: 64.2 us -> 73.8 us
    all_gather x1, waiting for transfers between devices: 100 us -> 0.01 us  [body(): portion = lax.all_gather(proj_heads, ('row', 'src'), axis=0, tiled=True)]
    ppermute x0 -> x3, waiting for transfers between devices: none -> 69.4 us  [body(): lax.ppermute(held, 'width', [(i, (i + 1) % n_dev) for i in range(n_dev)])]
    all_gather x1 -> x0, waiting for transfers between devices: 47.7 us -> none  [body(): weights = lax.all_gather(weights, 'width', axis=0, tiled=True)]
    unnamed x6 -> x14, local copies, waits for them, and re-layouts: 1.53 us -> 8.37 us
  transfers between devices with their start and end apart: 4 -> 6, of which waited for: 4 -> 5; matrix products, arithmetic and copies ran while one was open for 4% -> 10% of each run, Pallas kernels for 0% -> 0%
where the time goes in v1:
time: 369 us; the launch traced here: 368 us
  matrix products  123 us (33%)
  waiting for transfers between devices  81.8 us (22%)
  local copies, waits for them, and re-layouts  73.8 us (20%)
  other arithmetic  30.7 us (8%)
  loops' own time  22.2 us (6%)
  starting transfers between devices  14.1 us (4%)
  between operations  13.7 us (4%)
  blocking collectives  8.38 us (2%)
    dot_general x16, matrix products, compute(): jnp.einsum('hij,jhe->ije', attend, source_images, preferred_element_type=...  96.1 us
    ppermute x3, waiting for transfers between devices, body(): lax.ppermute(held, 'width', [(i, (i + 1) % n_dev) for i in range(n_dev)])  69.4 us
    while x2, local copies, waits for them, and re-layouts, body(): lax.fori_loop(0, turns, tile, jnp.zeros((row_count, col_count), jnp.float...  45.9 us
    dot_general x1, matrix products, body(): jnp.einsum('jhd,hde->jhe', chosen, portion, preferred_element_type=jnp.fl...  24.2 us
    another operation x1, loops' own time, body(): lax.fori_loop(0, turns, tile, jnp.zeros((row_count, col_count), jnp.float...  21.8 us
    dynamic_update_slice x16, local copies, waits for them, and re-layouts, tile(): return lax.dynamic_update_slice(running, result, (row_start, col_start))  13.7 us
    reduce_max x16, other arithmetic, tile(): jnp.max(row_slice) >= jnp.min(col_slice)  12.5 us
    all_to_all x2, starting transfers between devices, sent_to_all(): return lax.all_to_all(copies, axis, split_axis=0, concat_axis=0, tiled=True)  12.4 us
  transfers between devices with their start and end apart: 6, of which 5 were waited for; matrix products, arithmetic and copies ran while one was open for 10% of the time, Pallas kernels for 0%

profile of v1, /device:TPU:25, one launch (start us, length us, event | category | flops | bytes accessed | tf_op | source)
XLA Modules:
  0.0 367.6 jit_solution(17169989095466100934)
XLA Ops:
  25.4 24.6 %collective-permute-done = bf16[16,256,128]{2,1,0:T(8,128)(2,1)S(1)} collective-permute-done((bf16[16,256,128]{2,1,0:T(8,128)(2,1)S(1)}, bf16[16,256,128]{2,1,0:T(8,128)(2,1)S(1)}, u32[]{:S(2)}, u32[]{:S(2)}) %collective-permute-start) | collective-permute-done | bytes 1048608 | tf_op jit(solution)/shard_map/ppermute | solution.py:95
  50.0 24.3 %collective-permute-done.1 = bf16[16,256,128]{2,1,0:T(8,128)(2,1)} collective-permute-done((bf16[16,256,128]{2,1,0:T(8,128)(2,1)S(1)}, bf16[16,256,128]{2,1,0:T(8,128)(2,1)}, u32[]{:S(2)}, u32[]{:S(2)}) %collective-permute-start.1) | collective-permute-done | bytes 1048608 | tf_op jit(solution)/shard_map/ppermute | solution.py:95
  77.4 20.5 %collective-permute-done.2 = bf16[16,256,128]{2,1,0:T(8,128)(2,1)} collective-permute-done((bf16[16,256,128]{2,1,0:T(8,128)(2,1)}, bf16[16,256,128]{2,1,0:T(8,128)(2,1)}, u32[]{:S(2)}, u32[]{:S(2)}) %collective-permute-start.2) | collective-permute-done | bytes 1048608 | tf_op jit(solution)/shard_map/ppermute | solution.py:95
  109.6 15.9 %copy.29 = bf16[64,256,128]{0,1,2:T(8,128)(2,1)} copy(bf16[64,256,128]{2,1,0:T(8,128)(2,1)} %constant_dynamic-slice_fusion) | data formatting | bytes 8388608 | tf_op jit(solution)/shard_map/while | solution.py:141
  125.5 24.2 %convert_bitcast_fusion = bf16[128,64,2048]{2,0,1:T(8,128)(2,1)} fusion(bf16[64,128,2048]{2,1,0:T(8,128)(2,1)} %all-gather.2.cloned.1.call-done, bf16[128,64,128]{2,1,0:T(8,128)(2,1)S(1)} %copy-done.1), kind=kOutput, calls=%fused_computation.7 | convolution fusion | flops 4311744512 | bytes 69206016 | tf_op jit(solution)/shard_map/jhd,hde->jhe/dot_general | solution.py:111
  149.7 30.0 %copy.28 = bf16[128,64,2048]{2,1,0:T(8,128)(2,1)} copy(bf16[128,64,2048]{2,0,1:T(8,128)(2,1)} %convert_bitcast_fusion) | data formatting | bytes 67108864 | tf_op jit(solution)/shard_map/while | solution.py:141
  179.7 156.7 %while.15 = (s32[]{:T(128)}, f32[256,128]{0,1:T(8,128)S(1)}, s32[256]{0:T(256)S(1)}, s32[128]{0:T(128)S(1)}, bf16[128,64,2048]{2,1,0:T(8,128)(2,1)}, /*index=5*/...) while((s32[]{:T(128)}, f32[256,128]{0,1:T(8,128)S(1)}, ...), condition=%wide.region_8.9_spmd, body=%wide.region_2.8_spmd.sunk | while | flops 545257600 | bytes 8939898 | solution.py:141
  182.6 6.0 %conditional.2 = (f32[64,32]{0,1:T(8,128)S(1)}) conditional(s32[]{:T(128)} %convert_element_type.48, () %tuple.54, (s32[]{:T(128)}, bf16[128,64,2048]{2,1,0:T(8,128)(2,1)}, s32[]{:T(128)}, bf16[64,256,128]{0,1,2:T(8,128)(2,1)}) %tuple.55), branch_computations={%region_5.5_spmd, %region_6.7_spmd} | conditional | flops 545257472 | bytes 8922700 | solution.py:138
  192.4 6.0 %conditional.2 = (f32[64,32]{0,1:T(8,128)S(1)}) conditional(s32[]{:T(128)} %convert_element_type.48, () %tuple.54, (s32[]{:T(128)}, bf16[128,64,2048]{2,1,0:T(8,128)(2,1)}, s32[]{:T(128)}, bf16[64,256,128]{0,1,2:T(8,128)(2,1)}) %tuple.55), branch_computations={%region_5.5_spmd, %region_6.7_spmd} | conditional | flops 545257472 | bytes 8922700 | solution.py:138
  202.2 6.0 %conditional.2 = (f32[64,32]{0,1:T(8,128)S(1)}) conditional(s32[]{:T(128)} %convert_element_type.48, () %tuple.54, (s32[]{:T(128)}, bf16[128,64,2048]{2,1,0:T(8,128)(2,1)}, s32[]{:T(128)}, bf16[64,256,128]{0,1,2:T(8,128)(2,1)}) %tuple.55), branch_computations={%region_5.5_spmd, %region_6.7_spmd} | conditional | flops 545257472 | bytes 8922700 | solution.py:138
  212.0 6.0 %conditional.2 = (f32[64,32]{0,1:T(8,128)S(1)}) conditional(s32[]{:T(128)} %convert_element_type.48, () %tuple.54, (s32[]{:T(128)}, bf16[128,64,2048]{2,1,0:T(8,128)(2,1)}, s32[]{:T(128)}, bf16[64,256,128]{0,1,2:T(8,128)(2,1)}) %tuple.55), branch_computations={%region_5.5_spmd, %region_6.7_spmd} | conditional | flops 545257472 | bytes 8922700 | solution.py:138
  221.6 6.0 %conditional.2 = (f32[64,32]{0,1:T(8,128)S(1)}) conditional(s32[]{:T(128)} %convert_element_type.48, () %tuple.54, (s32[]{:T(128)}, bf16[128,64,2048]{2,1,0:T(8,128)(2,1)}, s32[]{:T(128)}, bf16[64,256,128]{0,1,2:T(8,128)(2,1)}) %tuple.55), branch_computations={%region_5.5_spmd, %region_6.7_spmd} | conditional | flops 545257472 | bytes 8922700 | solution.py:138
  231.6 6.0 %conditional.2 = (f32[64,32]{0,1:T(8,128)S(1)}) conditional(s32[]{:T(128)} %convert_element_type.48, () %tuple.54, (s32[]{:T(128)}, bf16[128,64,2048]{2,1,0:T(8,128)(2,1)}, s32[]{:T(128)}, bf16[64,256,128]{0,1,2:T(8,128)(2,1)}) %tuple.55), branch_computations={%region_5.5_spmd, %region_6.7_spmd} | conditional | flops 545257472 | bytes 8922700 | solution.py:138
  241.7 6.0 %conditional.2 = (f32[64,32]{0,1:T(8,128)S(1)}) conditional(s32[]{:T(128)} %convert_element_type.48, () %tuple.54, (s32[]{:T(128)}, bf16[128,64,2048]{2,1,0:T(8,128)(2,1)}, s32[]{:T(128)}, bf16[64,256,128]{0,1,2:T(8,128)(2,1)}) %tuple.55), branch_computations={%region_5.5_spmd, %region_6.7_spmd} | conditional | flops 545257472 | bytes 8922700 | solution.py:138
  251.8 6.0 %conditional.2 = (f32[64,32]{0,1:T(8,128)S(1)}) conditional(s32[]{:T(128)} %convert_element_type.48, () %tuple.54, (s32[]{:T(128)}, bf16[128,64,2048]{2,1,0:T(8,128)(2,1)}, s32[]{:T(128)}, bf16[64,256,128]{0,1,2:T(8,128)(2,1)}) %tuple.55), branch_computations={%region_5.5_spmd, %region_6.7_spmd} | conditional | flops 545257472 | bytes 8922700 | solution.py:138
  261.7 6.0 %conditional.2 = (f32[64,32]{0,1:T(8,128)S(1)}) conditional(s32[]{:T(128)} %convert_element_type.48, () %tuple.54, (s32[]{:T(128)}, bf16[128,64,2048]{2,1,0:T(8,128)(2,1)}, s32[]{:T(128)}, bf16[64,256,128]{0,1,2:T(8,128)(2,1)}) %tuple.55), branch_computations={%region_5.5_spmd, %region_6.7_spmd} | conditional | flops 545257472 | bytes 8922700 | solution.py:138
  271.3 6.0 %conditional.2 = (f32[64,32]{0,1:T(8,128)S(1)}) conditional(s32[]{:T(128)} %convert_element_type.48, () %tuple.54, (s32[]{:T(128)}, bf16[128,64,2048]{2,1,0:T(8,128)(2,1)}, s32[]{:T(128)}, bf16[64,256,128]{0,1,2:T(8,128)(2,1)}) %tuple.55), branch_computations={%region_5.5_spmd, %region_6.7_spmd} | conditional | flops 545257472 | bytes 8922700 | solution.py:138
  280.9 6.0 %conditional.2 = (f32[64,32]{0,1:T(8,128)S(1)}) conditional(s32[]{:T(128)} %convert_element_type.48, () %tuple.54, (s32[]{:T(128)}, bf16[128,64,2048]{2,1,0:T(8,128)(2,1)}, s32[]{:T(128)}, bf16[64,256,128]{0,1,2:T(8,128)(2,1)}) %tuple.55), branch_computations={%region_5.5_spmd, %region_6.7_spmd} | conditional | flops 545257472 | bytes 8922700 | solution.py:138
  290.4 6.0 %conditional.2 = (f32[64,32]{0,1:T(8,128)S(1)}) conditional(s32[]{:T(128)} %convert_element_type.48, () %tuple.54, (s32[]{:T(128)}, bf16[128,64,2048]{2,1,0:T(8,128)(2,1)}, s32[]{:T(128)}, bf16[64,256,128]{0,1,2:T(8,128)(2,1)}) %tuple.55), branch_computations={%region_5.5_spmd, %region_6.7_spmd} | conditional | flops 545257472 | bytes 8922700 | solution.py:138
  319.6 6.0 %conditional.2 = (f32[64,32]{0,1:T(8,128)S(1)}) conditional(s32[]{:T(128)} %convert_element_type.48, () %tuple.54, (s32[]{:T(128)}, bf16[128,64,2048]{2,1,0:T(8,128)(2,1)}, s32[]{:T(128)}, bf16[64,256,128]{0,1,2:T(8,128)(2,1)}) %tuple.55), branch_computations={%region_5.5_spmd, %region_6.7_spmd} | conditional | flops 545257472 | bytes 8922700 | solution.py:138
  329.5 6.0 %conditional.2 = (f32[64,32]{0,1:T(8,128)S(1)}) conditional(s32[]{:T(128)} %convert_element_type.48, () %tuple.54, (s32[]{:T(128)}, bf16[128,64,2048]{2,1,0:T(8,128)(2,1)}, s32[]{:T(128)}, bf16[64,256,128]{0,1,2:T(8,128)(2,1)}) %tuple.55), branch_computations={%region_5.5_spmd, %region_6.7_spmd} | conditional | flops 545257472 | bytes 8922700 | solution.py:138
  336.3 8.4 %all_to_all.16 = f32[4,256,32]{1,2,0:T(8,128)S(1)} all-to-all(f32[4,256,32]{1,2,0:T(8,128)S(1)} %bitcast.40), channel_id=1, replica_groups=mesh['width'=4,'row'=4,'src'=8] {'width'}, dimensions={0} | all-to-all | bytes 262144 | tf_op jit(solution)/shard_map/all_to_all | solution.py:55
  345.4 7.4 %all-to-all-start.2 = ((f32[32,1,256]{2,1,0:T(1,128)}), f32[32,1,256]{2,1,0:T(1,128)S(1)}, u32[]{:S(2)}, u32[]{:S(2)}) async-start(f32[32,1,256]{2,1,0:T(1,128)} %broadcast_in_dim.46), calls=%async_computation.2 | async-start | bytes 65536 | tf_op jit(solution)/shard_map/all_to_all | solution.py:14
  352.8 7.2 %all-to-all-done.2 = f32[32,1,256]{2,1,0:T(1,128)S(1)} async-done(((f32[32,1,256]{2,1,0:T(1,128)}), f32[32,1,256]{2,1,0:T(1,128)S(1)}, u32[]{:S(2)}, u32[]{:S(2)}) %all-to-all-start.2) | async-done | bytes 32800 | tf_op jit(solution)/shard_map/all_to_all | solution.py:14
  (114 shorter events, 181.3 us)
Async XLA Ops:
  6.5 2.2 copy-start.2
  6.5 119.0 %all-gather.2.cloned.1.call-start = ((), (), s32[]{:S(2)}) async-start(), calls=%async_computation.3 | async-start | bytes 34603008 | tf_op jit(solution)/shard_map/all_gather | solution.py:102
  9.5 6.5 %copy-start = (f32[2,128,256,8]{2,1,3,0:T(8,128)}, f32[2,128,256,8]{2,1,3,0:T(8,128)S(1)}, u32[]{:S(2)}) copy-start(f32[2,128,256,8]{2,1,3,0:T(8,128)S(1)} %get-tuple-element.232) | copy-start | bytes 6291460
  10.9 11.5 %all-to-all-start = ((f32[8,32,256]{2,1,0:T(8,128)}), f32[8,32,256]{2,1,0:T(8,128)S(1)}, u32[]{:S(2)}, u32[]{:S(2)}) async-start(f32[8,32,256]{2,1,0:T(8,128)} %broadcast_in_dim.44), calls=%async_computation | async-start | bytes 524288 | tf_op jit(solution)/shard_map/all_to_all | solution.py:14
  23.7 26.3 %collective-permute-start = (bf16[16,256,128]{2,1,0:T(8,128)(2,1)S(1)}, bf16[16,256,128]{2,1,0:T(8,128)(2,1)S(1)}, u32[]{:S(2)}, u32[]{:S(2)}) collective-permute-start(bf16[16,256,128]{2,1,0:T(8,128)(2,1)S(1)} %select_convert_fusion), channel_id=1, source_target_pairs={{0,32},{32,64},{64,96},{96,0},{1,33},{33,65},{65,97},{97,1},{2,34}... | collective-permute-start | bytes 3145736 | tf_op jit(solution)/shard_map/ppermute | solution.py:95
  50.0 24.3 %collective-permute-start.1 = (bf16[16,256,128]{2,1,0:T(8,128)(2,1)S(1)}, bf16[16,256,128]{2,1,0:T(8,128)(2,1)}, u32[]{:S(2)}, u32[]{:S(2)}) collective-permute-start(bf16[16,256,128]{2,1,0:T(8,128)(2,1)S(1)} %collective-permute-done), channel_id=1, source_target_pairs={{0,32},{32,64},{64,96},{96,0},{1,33},{33,65},{65,97},{97,1},{2,34}... | collective-permute-start | bytes 3145736 | tf_op jit(solution)/shard_map/ppermute | solution.py:95
  74.4 23.6 %collective-permute-start.2 = (bf16[16,256,128]{2,1,0:T(8,128)(2,1)}, bf16[16,256,128]{2,1,0:T(8,128)(2,1)}, u32[]{:S(2)}, u32[]{:S(2)}) collective-permute-start(bf16[16,256,128]{2,1,0:T(8,128)(2,1)} %collective-permute-done.1), channel_id=1, source_target_pairs={{0,32},{32,64},{64,96},{96,0},{1,33},{33,65},{65,97},{97,1},{2,34}... | collective-permute-start | bytes 3145736 | tf_op jit(solution)/shard_map/ppermute | solution.py:95
  109.6 15.9 %copy-start.1 = (bf16[128,64,128]{2,1,0:T(8,128)(2,1)S(1)}, bf16[128,64,128]{2,1,0:T(8,128)(2,1)}, u32[]{:S(2)}) copy-start(bf16[128,64,128]{2,1,0:T(8,128)(2,1)} %convert_bitcast_fusion.1) | copy-start | bytes 6291460
  345.4 14.6 %all-to-all-start.2 = ((f32[32,1,256]{2,1,0:T(1,128)}), f32[32,1,256]{2,1,0:T(1,128)S(1)}, u32[]{:S(2)}, u32[]{:S(2)}) async-start(f32[32,1,256]{2,1,0:T(1,128)} %broadcast_in_dim.46), calls=%async_computation.2 | async-start | bytes 65536 | tf_op jit(solution)/shard_map/all_to_all | solution.py:14
Sparse Core Ops, SparseCore 0:
  9.6 115.4 all-gather.1
